TPU v7x, 512 devices: a whole 4x4x16 slice. The times are simulated.
512 devices in a mesh: seq: 16 (over z), head: 32 (over x, y, core).
Axes of the slice: x: 4, y: 4, z: 16, core: 2. Of those that a mesh axis runs over, the one named last changes fastest.
Arguments:
- queries: bfloat16 [32768, 8192], P('seq', 'head'), may hold values from -6 to 6
- key_rows: bfloat16 [32768, 8192], P('seq', 'head'), may hold values from -0.52734375 to 0.52734375
- value_rows: bfloat16 [32768, 8192], P('seq', 'head')
- log_decay: float32 [64, 32768], P('head', 'seq')
- norm_gain: float32 [8192], P('head'), may hold values from 0.1 to 1.9
- lengths: int32 [48], replicated, may hold values from 1 to 4095, as said below
- decode_slot: int32 [48], replicated, may hold values from 0 to 47, each once
Outputs:
- attended: bfloat16 [32768, 8192], P('seq', 'head')
- final_states: float32 [48, 64, 128, 128], P('seq', 'head')
Inputs may be any that keep to these rules, and one draw needn't show every extreme that they name: The lengths sum to 32768. Every block of 2048 consecutive positions (one index of seq) holds between 1 and 5 last positions of prompts; the last position of the pack ends a prompt; in every draw some block holds 5 and some holds 1. `decode_slot`: each row of final_states is named once; rows j * 3 to j * 3 + 2 lie on index j of seq.
All inputs are finite; a program needn't handle non-finite values.
Results may differ from a plain program's by a relative error of at most 0.0075.
Values sent between devices are 32-bit elements; how exact they have to be, the bound alone decides.
A program may use at most 64 MiB of HBM per device.

v0:
```python
import functools

import jax
import jax.numpy as jnp
from jax import lax
from jax.experimental import pallas as pl
from jax.experimental.pallas import tpu as pltpu
from jax.sharding import PartitionSpec as P

DK = 128
DV = 128
CHUNK = 256
SLOTS = 3
ENDS = 5
LANES = 128
LONGEST = 32
LENGTHS = (9, 10, 11, 12, 13, 14, 16, LONGEST)
PIECES = 4
FAR = 1 << 20
NEG = -1e30
EPSILON = 1e-06
MESH = pl.DeviceIdType.MESH
F32 = jnp.float32
BF16 = jnp.bfloat16
SORT5 = ((0, 1), (3, 4), (2, 4), (2, 3), (1, 4), (0, 3), (0, 2), (1, 3), (1, 2))
PRECISE = lax.Precision.HIGHEST


def iota(shape, axis):
    return lax.broadcasted_iota(jnp.int32, shape, axis)


def halves(wide, axis):
    upper = wide.astype(BF16)
    lower = (wide - upper.astype(F32)).astype(BF16)
    return jnp.concatenate([upper, lower], axis=axis)


def outer_sum(scaled_keys, values):
    both = lax.dot_general(
        halves(scaled_keys, 1), values, (((0,), (0,)), ((), ())), preferred_element_type=F32
    )
    return both[:DK] + both[DK:]


def query_state(rows, state_halves):
    both = jnp.dot(rows, state_halves, preferred_element_type=F32)
    return both[:, :DV] + both[:, DV:]


def route(me, ring, tok, prompts, finish, slot_ref, plan):
    shape = (8, LANES)
    sub, lane = iota(shape, 0), iota(shape, 1)
    place = lane & (ring - 1)
    leftward = (sub & 1) == 1
    dev = jnp.where(leftward, (ring - place) & (ring - 1), place)
    candidate = (lane // ring) * 4 + (sub >> 1)
    start = dev * tok
    first = jnp.zeros(shape, jnp.int32)
    for p in range(prompts):
        first = first + jnp.where(finish[p] < start, 1, 0)
    items = [jnp.zeros(shape, jnp.int32)] * ENDS
    for p in range(prompts):
        slot = slot_ref[p]
        owner = (slot * 43) >> 7
        value = owner * 4 + (slot - owner * SLOTS) + 1
        here = (finish[p] >= start) & (finish[p] < start + tok)
        rank = jnp.where(here, p - first, -1)
        items = [jnp.where(rank == k, value, item) for k, item in enumerate(items)]
    keys, own = [], []
    half = ring // 2
    for k, item in enumerate(items):
        owner, row = (item - 1) >> 2, (item - 1) & 3
        right = (owner - dev) & (ring - 1)
        left = (ring - right) & (ring - 1)
        mixed_bits = ((item * 37 + candidate * 1013 + 7) * 40503) >> 9
        draw = (mixed_bits ^ (mixed_bits >> 5)) & 7
        free = draw < jnp.where(right == half - 1, 6, jnp.where(right == half, 4, 2))
        fixed = (right < half) | ((right == half) & ((item & 1) == 0))
        near = (right >= half - 1) & (right <= half + 1) & (candidate > 0)
        go_right = (near & free) | (jnp.logical_not(near) & fixed)
        turned = (go_right & jnp.logical_not(leftward)) | (jnp.logical_not(go_right) & leftward)
        chosen = (item > 0) & (right > 0) & turned
        distance = jnp.where(leftward, left, right)
        keys.append(jnp.where(chosen, distance * 64 + k * 8 + row, 0))
        own.append(jnp.where((item > 0) & (right == 0), row + 1, 0))
    for a, b in SORT5:
        keys[a], keys[b] = jnp.maximum(keys[a], keys[b]), jnp.minimum(keys[a], keys[b])

    def turn(value, shift):
        wrapped = pltpu.roll(value, LANES - ring + shift, 1)
        return jnp.where(place < shift, wrapped, pltpu.roll(value, shift, 1))

    zero = jnp.zeros(shape, jnp.int32)
    belt, last = zero, zero
    for t in range(LONGEST):
        if t == 0:
            second = ((keys[0] >> 3) & 7) == 0
            riding = jnp.where(second, keys[1], keys[0])
            board = leftward & (riding > 0)
            following = [jnp.where(second, keys[0], keys[1])] + keys[2:] + [zero]
        else:
            riding = keys[0]
            board = (belt == 0) & (riding > 0)
            following = keys[1:] + [zero]
        boarded = jnp.where(board, ((riding >> 3) & 7) + 1, 0)
        belt = jnp.where(board, riding, belt)
        keys = [jnp.where(board, new, old) for new, old in zip(following, keys)]
        last = jnp.where(belt > 0, t + 1, last)
        moved = jnp.where(belt >= 128, belt - 64, jnp.where(belt >= 64, (belt & 7) + 1, 0))
        moved = turn(moved, 1)
        taken = jnp.where(moved < 64, moved, 0)
        belt = jnp.where(moved >= 64, moved, 0)
        plan[t] = boarded * 4 + taken
    shift = 1
    while shift < ring:
        last = jnp.maximum(last, turn(last, shift))
        shift *= 2
    other = jnp.where(leftward, pltpu.roll(last, 1, 0), pltpu.roll(last, 7, 0))
    best = jnp.min(jnp.maximum(last, other) * 32 + candidate)
    mirror = jnp.where(leftward, (ring - me) & (ring - 1), me)
    mine = (candidate == (best & 31)) & (place == mirror)
    tiles = [jnp.where(mine, plan[t], 0) for t in range(LONGEST)]
    tiles += [jnp.where(mine & jnp.logical_not(leftward), item, 0) for item in own]
    tiles += [zero] * (-len(tiles) % 16)
    stacked = jnp.concatenate(tiles, axis=0).astype(F32).astype(BF16)
    rows = stacked.shape[0]
    wide = jnp.dot(stacked, jnp.ones((LANES, LANES), BF16), preferred_element_type=F32)
    r0, r1 = iota((rows, rows), 0), iota((rows, rows), 1)
    gather = (((r0 ^ r1) & ~7) == 0) & (((r0 ^ r1) & 1) == 0)
    table = jnp.dot(
        gather.astype(F32).astype(BF16), wide.astype(BF16), preferred_element_type=F32
    )
    return table, best >> 5


def table_rows():
    return (-(-(LONGEST + ENDS) // 16) * 16) * 8


def index_of(positions, ends):
    index = jnp.where(positions > ends[0], 1, 0)
    for end in ends[1:]:
        index = index + jnp.where(positions > end, 1, 0)
    return index


def decay_parts(run_row, run_col, c, h, heads):
    per = CHUNK // LANES
    base = pl.multiple_of(c * CHUNK, CHUNK)
    col = run_col[pl.ds(base, CHUNK), h : h + 1]
    row = jnp.concatenate(
        [run_row[pl.ds((per * c + i) * heads + h, 1), :] for i in range(per)], axis=1
    )
    prior = run_row[pl.ds(jnp.maximum(per * c - 1, 0) * heads + h, 1), :]
    at_entry = jnp.where(c > 0, prior[:, LANES - 1 :], 0.0)
    return col, row, at_entry


def local_kernel(
    ring,
    len_hbm,
    slot_hbm,
    decay_hbm,
    k_hbm,
    v_hbm,
    held_ref,
    ends_ref,
    tail_ref,
    table_ref,
    first_ref,
    run_row,
    run_col,
    ends_out,
    branch_ref,
    len_ref,
    slot_ref,
    decay_ref,
    k_ref,
    v_ref,
    state,
    plan,
    finish_s,
    sems,
):
    tok = k_ref.shape[0]
    heads = decay_ref.shape[0]
    prompts = len_ref.shape[0]
    tiles = tok // LANES
    copies = [
        pltpu.make_async_copy(src, dst, sems.at[i])
        for i, (src, dst) in enumerate(
            [
                (len_hbm, len_ref),
                (slot_hbm, slot_ref),
                (decay_hbm, decay_ref),
                (k_hbm, k_ref),
                (v_hbm, v_ref),
            ]
        )
    ]
    for copy in copies:
        copy.start()
    me = lax.axis_index("seq")
    anchor = me * tok
    square = (LANES, LANES)
    copies[0].wait()
    copies[1].wait()
    copies[2].wait()

    decay = decay_ref[...]
    rows = jnp.concatenate(
        [decay[:, c * LANES : (c + 1) * LANES] for c in range(tiles)], axis=0
    )
    upper = (iota(square, 0) <= iota(square, 1)).astype(F32)
    within = jnp.dot(rows, upper, precision=PRECISE, preferred_element_type=F32)
    count = tiles * heads
    wide = jnp.concatenate([within, jnp.zeros((LANES - count, LANES), F32)], axis=0)
    totals = jnp.broadcast_to(wide[:, LANES - 1 :], square)
    earlier = (iota(square, 1) < iota(square, 0)) & (
        ((iota(square, 0) - iota(square, 1)) & (heads - 1)) == 0
    )
    running = wide + jnp.dot(
        earlier.astype(F32), totals, precision=PRECISE, preferred_element_type=F32
    )
    run_row[...] = running
    turned = running.T
    for c in range(tiles):
        shift = (LANES - heads * c) % LANES
        run_col[c * LANES : (c + 1) * LANES, :] = (
            pltpu.roll(turned, shift, 1) if shift else turned
        )

    total = jnp.int32(0)
    before = jnp.int32(0)
    ended = jnp.int32(0)
    finish = []
    for p in range(prompts):
        total = total + len_ref[p]
        finish.append(total - 1)
        finish_s[p] = total - 1
        before = before + jnp.where(total - 1 < anchor, 1, 0)
        ended = ended + jnp.where(total - 1 < anchor + tok, 1, 0)
    ended = ended - before
    ends = []
    for k in range(ENDS):
        place = finish_s[jnp.minimum(before + k, prompts - 1)] - anchor
        ends.append(jnp.where(k < ended, place, FAR))
        ends_out[k] = ends[k]

    table, steps = route(me, ring, tok, prompts, finish, slot_ref, plan)
    boards = jnp.floor(table * 0.25)
    table_ref[0] = boards
    table_ref[1] = table - 4.0 * boards
    branch = jnp.int32(0)
    for length in LENGTHS[:-1]:
        branch = branch + jnp.where(steps > length, 1, 0)
    branch_ref[0] = branch

    at_end = jnp.where(
        (iota(square, 0) // heads) * LANES + iota(square, 1) == ends[0], running, 0.0
    )
    for h in range(heads):
        head_rows = (iota(square, 0) & (heads - 1)) == h
        first = jnp.sum(jnp.where(head_rows, at_end, 0.0), keepdims=True)
        first_ref[h : h + 1, :] = jnp.exp(jnp.broadcast_to(first, (1, LANES)))

    copies[3].wait()
    copies[4].wait()
    ends_ref[...] = jnp.zeros_like(ends_ref)

    def chunk(c, held):
        base = pl.multiple_of(c * CHUNK, CHUNK)
        span = pl.ds(base, CHUNK)
        index_col = index_of(base + iota((CHUNK, 1), 0), ends)
        entry = index_of(base - 1, ends)
        last = index_of(base + CHUNK - 1, ends)
        following = []
        for h in range(heads):
            cols = slice(h * DK, (h + 1) * DK)
            col, row, at_entry = decay_parts(run_row, run_col, c, h, heads)
            at_last = row[:, CHUNK - 1 :]
            state[c, h] = held[h]
            held_ref[c, h] = halves(held[h], 1)
            weight = jnp.exp(jnp.where(index_col == last, at_last - col, NEG))
            keep = jnp.exp(jnp.where(entry == last, at_last - at_entry, NEG))
            fresh = outer_sum(k_ref[span, cols].astype(F32) * weight, v_ref[span, cols])
            following.append(keep * held[h] + fresh)
        return tuple(following)

    empty = tuple(jnp.zeros((DK, DV), F32) for _ in range(heads))
    held = lax.fori_loop(0, tok // CHUNK, chunk, empty)
    open_end = index_of(jnp.int32(tok - 1), ends) == ended
    for h in range(heads):
        tail_ref[h] = jnp.where(open_end, held[h], 0.0)

    def one_end(k, carry):
        place = finish_s[before + k] - anchor
        c = place // CHUNK
        base = pl.multiple_of(c * CHUNK, CHUNK)
        span = pl.ds(base, CHUNK)
        index_col = index_of(base + iota((CHUNK, 1), 0), ends)
        entry = index_of(base - 1, ends)
        here = base + iota((1, CHUNK), 1) == place
        for h in range(heads):
            cols = slice(h * DK, (h + 1) * DK)
            col, row, at_entry = decay_parts(run_row, run_col, c, h, heads)
            at_end = jnp.sum(jnp.where(here, row, 0.0), axis=1, keepdims=True)
            weight = jnp.exp(jnp.where(index_col == k, at_end - col, NEG))
            keep = jnp.exp(jnp.where(entry == k, at_end - at_entry, NEG))
            fresh = outer_sum(k_ref[span, cols].astype(F32) * weight, v_ref[span, cols])
            ends_ref[k, h] = keep * state[c, h] + fresh
        return carry

    lax.fori_loop(0, ended, one_end, 0)


def grid_of(head_size):
    return (4, 4, 2) if head_size == 32 else (1, 1, head_size)


def ring_kernel(
    steps,
    sizes,
    ends_s,
    q_hbm,
    k_hbm,
    v_hbm,
    held_ref,
    ends_in,
    tail_ref,
    table_ref,
    first_ref,
    run_row,
    run_col,
    gain_ref,
    attended_ref,
    final_ref,
    q_ref,
    k_ref,
    v_ref,
    ends_ref,
    mixed,
    sums,
    got,
    came,
    sent,
    load_sems,
    send_sem,
    recv_sem,
    sum_send,
    sum_recv,
):
    ring, head_size = sizes
    nx, ny, nc = grid_of(head_size)
    tok, width = q_ref.shape
    heads = width // DV
    tiles = tok // LANES
    piece = DK // PIECES
    loads = [
        pltpu.make_async_copy(src, dst, load_sems.at[i])
        for i, (src, dst) in enumerate([(q_hbm, q_ref), (k_hbm, k_ref), (v_hbm, v_ref)])
    ]
    for load in loads:
        load.start()
    z = lax.axis_index("seq")
    lane_id = lax.axis_index("head")
    core = lax.rem(lane_id, nc)
    y = lax.rem(lane_id // nc, ny)
    x = lane_id // (nc * ny)
    ahead = (lax.rem(z + 1, ring), lane_id)
    behind = (lax.rem(z + ring - 1, ring), lane_id)
    towards = (ahead, behind)
    stages = [
        [(z, (x * ny + y) * nc + lax.rem(core + d, nc)) for d in range(1, nc)],
        [(z, (lax.rem(x + d, nx) * ny + y) * nc + core) for d in range(1, nx)],
        [(z, (x * ny + lax.rem(y + d, ny)) * nc + core) for d in range(1, ny)],
    ]
    peers = [ahead, behind] + [peer for stage in stages for peer in stage]
    barrier = pltpu.get_barrier_semaphore()
    for peer in peers:
        pl.semaphore_signal(barrier, inc=1, device_id=peer, device_id_type=MESH)
    pl.semaphore_wait(barrier, len(peers))

    parts = [(h, i, slice(i * piece, (i + 1) * piece)) for h in range(heads) for i in range(PIECES)]

    def belt_copy(way, t, h, i, source=None):
        rows = slice(i * piece, (i + 1) * piece)
        return pltpu.make_async_remote_copy(
            src_ref=sent.at[way, t, h, rows] if source is None else source.at[h, rows],
            dst_ref=came.at[way, t, h, rows],
            send_sem=send_sem.at[way, t, h, i],
            recv_sem=recv_sem.at[way, t, h, i],
            device_id=towards[way],
            device_id_type=MESH,
        )

    def sum_copies(stage):
        base = sum(len(s) for s in stages[:stage])
        return [
            pltpu.make_async_remote_copy(
                src_ref=sums.at[stage],
                dst_ref=got.at[base + i],
                send_sem=sum_send.at[base + i],
                recv_sem=sum_recv.at[base + i],
                device_id=peer,
                device_id_type=MESH,
            )
            for i, peer in enumerate(stages[stage])
        ]

    def board_row(t, way):
        return table_ref[0, pl.ds(t * 8 + way, 1), :]

    def take_row(t, way):
        return table_ref[1, pl.ds(t * 8 + way, 1), :]

    def send_piece(way, t, part, value, source, lowest):
        h, i, rows = part
        board = board_row(t, way)
        for k in range(lowest, ENDS):
            value = jnp.where(board == float(k + 1), source[k, h, rows], value)
        sent[way, t, h, rows] = value
        belt_copy(way, t, h, i).start()

    def take_piece(way, t, part):
        h, i, rows = part
        value = came[way, t, h, rows]
        take = take_row(t, way)
        for row in range(SLOTS):
            final_ref[row, h, rows] = jnp.where(
                take == float(row + 1), value, final_ref[row, h, rows]
            )

    for h, i, rows in parts:
        belt_copy(0, 0, h, i, tail_ref).start()
    for part in parts:
        send_piece(1, 0, part, ends_in[0, part[0], part[2]], ends_in, 1)
    for k in range(1, ENDS):
        ends_ref[k] = ends_in[k]
    for load in loads:
        load.wait()
    for h, i, rows in parts:
        belt_copy(0, 0, h, i, tail_ref).wait_recv()
        ends_ref[0, h, rows] = ends_in[0, h, rows] + first_ref[h : h + 1, :] * came[0, 0, h, rows]
    for row in range(SLOTS):
        for h in range(heads):
            value = jnp.zeros((DK, DV), F32)
            for k in range(ENDS):
                kept = table_ref[1, (LONGEST + k) * 8 : (LONGEST + k) * 8 + 1, :]
                value = jnp.where(kept == float(row + 1), ends_ref[k, h], value)
            final_ref[row, h] = value

    ends = [ends_s[k] for k in range(ENDS)]
    block = (CHUNK, CHUNK)

    def attend(c):
        base = pl.multiple_of(c * CHUNK, CHUNK)
        span = pl.ds(base, CHUNK)
        index_col = index_of(base + iota((CHUNK, 1), 0), ends)
        index_row = index_of(base + iota((1, CHUNK), 1), ends)
        entry = index_of(base - 1, ends)
        linked = (index_col == index_row) & (iota(block, 0) >= iota(block, 1))
        for h in range(heads):
            cols = slice(h * DK, (h + 1) * DK)
            col, row, at_entry = decay_parts(run_row, run_col, c, h, heads)
            query = q_ref[span, cols]
            scores = lax.dot_general(
                query, k_ref[span, cols], (((1,), (1,)), ((), ())), preferred_element_type=F32
            )
            weights = (scores * jnp.exp(jnp.where(linked, col - row, NEG))).astype(BF16)
            inside = jnp.dot(weights, v_ref[span, cols], preferred_element_type=F32)
            reach = jnp.exp(jnp.where(index_col == entry, col - at_entry, NEG))
            through = query_state(query, held_ref[c, h])
            from_start = jnp.exp(jnp.where(index_col == 0, col, NEG))
            carried = query_state(query, halves(came[0, 0, h], 1))
            mixed[span, cols] = inside + through * reach + carried * from_start

    def square_sums(c, carry):
        per = CHUNK // LANES
        span = pl.ds(pl.multiple_of(c * CHUNK, CHUNK), CHUNK)
        whole = mixed[span, :]
        row_sums = lax.dot_general(
            jnp.ones((8, 2 * width), BF16),
            halves(whole * whole, 1),
            (((1,), (1,)), ((), ())),
            preferred_element_type=F32,
        )
        for i in range(per):
            sums[0, pl.ds(c * per + i, 1), :] = row_sums[:1, i * LANES : (i + 1) * LANES]
        return carry

    def start_sums(stage):
        for copy in sum_copies(stage):
            copy.start()

    def join_sums(stage):
        base = sum(len(s) for s in stages[:stage])
        value = sums[stage]
        for i, copy in enumerate(sum_copies(stage)):
            copy.wait()
            value = value + got[base + i]
        sums[stage + 1] = value

    def normalize():
        mean = sums[3] * (1.0 / (width * head_size))
        inverse = lax.rsqrt(mean + EPSILON)
        turned = jnp.concatenate(
            [inverse, jnp.zeros((LANES - tiles, LANES), F32)], axis=0
        ).T
        gain = gain_ref[...]
        for c in range(tiles):
            span = slice(c * LANES, (c + 1) * LANES)
            scaled = mixed[span, :] * turned[:, c : c + 1] * gain
            attended_ref[span, :] = scaled.astype(BF16)

    chunks = tok // CHUNK
    each = chunks // 4

    def step(t, carry):
        for part in parts:
            h, i, rows = part
            for way in range(2):
                if way == 0:

                    @pl.when(t > 1)
                    def _():
                        belt_copy(0, t - 1, h, i).wait_recv()
                else:
                    belt_copy(1, t - 1, h, i).wait_recv()
                send_piece(way, t, part, came[way, t - 1, h, rows], ends_ref, 0)
        for part in parts:
            for way in range(2):
                take_piece(way, t - 1, part)

        @pl.when(t <= 4)
        def _():
            def some(j, inner):
                attend((t - 1) * each + j)
                return inner

            lax.fori_loop(0, each, some, 0)

        @pl.when(t == 5)
        def _():
            lax.fori_loop(0, chunks, square_sums, 0)
            start_sums(0)

        @pl.when(t == 6)
        def _():
            join_sums(0)
            start_sums(1)

        @pl.when(t == 7)
        def _():
            join_sums(1)
            start_sums(2)

        @pl.when(t == 8)
        def _():
            join_sums(2)
            normalize()

        return carry

    lax.fori_loop(1, steps, step, 0)
    for part in parts:
        h, i, rows = part
        for way in range(2):
            belt_copy(way, steps - 1, h, i).wait_recv()
            take_piece(way, steps - 1, part)

    def drain(t, carry):
        for h, i, rows in parts:
            for way in range(2):
                belt_copy(way, t, h, i).wait_send()
        return carry

    lax.fori_loop(0, steps, drain, 0)


def store_kernel(attended, final, attended_hbm, final_hbm, sems):
    first = pltpu.make_async_copy(attended, attended_hbm, sems.at[0])
    second = pltpu.make_async_copy(final, final_hbm, sems.at[1])
    first.start()
    second.start()
    first.wait()
    second.wait()


def vmem(count):
    return [pl.BlockSpec(memory_space=pltpu.VMEM)] * count


def hbm(count):
    return [pl.BlockSpec(memory_space=pltpu.HBM)] * count


def solution(mesh):
    ring = mesh.shape["seq"]
    head_size = mesh.shape["head"]
    nx, ny, nc = grid_of(head_size)
    hops = (nc - 1) + (nx - 1) + (ny - 1)

    def shards(queries, key_rows, value_rows, log_decay, norm_gain, lengths, decode_slot):
        tok, width = queries.shape
        heads = log_decay.shape[0]
        tiles = tok // LANES
        prompts = lengths.shape[0]
        shape = jax.ShapeDtypeStruct
        smem = pl.BlockSpec(memory_space=pltpu.SMEM)
        chunks = tok // CHUNK
        *local, ends, branch = pl.pallas_call(
            functools.partial(local_kernel, ring),
            out_shape=(
                shape((chunks, heads, DK, 2 * DV), BF16),
                shape((ENDS, heads, DK, DV), F32),
                shape((heads, DK, DV), F32),
                shape((2, table_rows(), LANES), F32),
                shape((8, LANES), F32),
                shape((LANES, LANES), F32),
                shape((tok, LANES), F32),
                shape((ENDS,), jnp.int32),
                shape((1,), jnp.int32),
            ),
            in_specs=hbm(5),
            out_specs=tuple(vmem(7)) + (smem, smem),
            scratch_shapes=[
                pltpu.SMEM((prompts,), jnp.int32),
                pltpu.SMEM((prompts,), jnp.int32),
                pltpu.VMEM((heads, tok), F32),
                pltpu.VMEM((tok, width), BF16),
                pltpu.VMEM((tok, width), BF16),
                pltpu.VMEM((chunks, heads, DK, DV), F32),
                pltpu.VMEM((LONGEST, 8, LANES), jnp.int32),
                pltpu.SMEM((prompts,), jnp.int32),
                pltpu.SemaphoreType.DMA((5,)),
            ],
            compiler_params=pltpu.CompilerParams(vmem_limit_bytes=40 << 20),
            name="local",
        )(lengths, decode_slot, log_decay, key_rows, value_rows)

        outs = (shape((tok, width), BF16), shape((SLOTS, heads, DK, DV), F32))

        def exchange(index, steps):
            belt = (2, steps, heads)
            ring_call = pl.pallas_call(
                functools.partial(ring_kernel, steps, (ring, head_size)),
                out_shape=outs,
                in_specs=[smem] + hbm(3) + vmem(8),
                out_specs=tuple(vmem(2)),
                scratch_shapes=[
                    pltpu.VMEM((tok, width), BF16),
                    pltpu.VMEM((tok, width), BF16),
                    pltpu.VMEM((tok, width), BF16),
                    pltpu.VMEM((ENDS, heads, DK, DV), F32),
                    pltpu.VMEM((tok, width), F32),
                    pltpu.VMEM((4, tiles, LANES), F32),
                    pltpu.VMEM((max(hops, 1), tiles, LANES), F32),
                    pltpu.VMEM(belt + (DK, DV), F32),
                    pltpu.VMEM(belt + (DK, DV), F32),
                    pltpu.SemaphoreType.DMA((3,)),
                    pltpu.SemaphoreType.DMA(belt + (PIECES,)),
                    pltpu.SemaphoreType.DMA(belt + (PIECES,)),
                    pltpu.SemaphoreType.DMA((max(hops, 1),)),
                    pltpu.SemaphoreType.DMA((max(hops, 1),)),
                ],
                compiler_params=pltpu.CompilerParams(
                    vmem_limit_bytes=48 << 20, collective_id=index, has_side_effects=True
                ),
                name=f"ring{steps}",
            )
            store_call = pl.pallas_call(
                store_kernel,
                out_shape=outs,
                in_specs=vmem(2),
                out_specs=tuple(hbm(2)),
                scratch_shapes=[pltpu.SemaphoreType.DMA((2,))],
                compiler_params=pltpu.CompilerParams(vmem_limit_bytes=4 << 20),
                name="store",
            )
            return lambda *operands: store_call(*ring_call(*operands))

        return lax.switch(
            branch[0],
            [exchange(index, steps) for index, steps in enumerate(LENGTHS)],
            ends,
            queries,
            key_rows,
            value_rows,
            *local,
            norm_gain.reshape(1, width),
        )

    in_specs = (
        P("seq", "head"),
        P("seq", "head"),
        P("seq", "head"),
        P("head", "seq"),
        P("head"),
        P(),
        P(),
    )
    out_specs = (P("seq", "head"), P("seq", "head", None, None))
    return jax.shard_map(shards, mesh=mesh, in_specs=in_specs, out_specs=out_specs, check_vma=False)
```

profile of v0, /device:TPU:8, one launch (start us, length us, event | category | flops | bytes accessed | tf_op | source)
XLA Modules:
  0.0 78.1 jit_solution(4900144984354771860)
XLA Ops:
  0.6 0.0 copy-start.2
  0.6 0.0 copy-start.1
  0.7 0.6 copy-done.2
  1.3 0.0 copy-done.1
  1.3 0.0 copy-start
  1.3 0.7 copy-done
  2.0 0.0 copy-start.3
  2.0 0.0 copy-start.4
  2.0 10.8 %local.1 = (bf16[8,2,128,256]{3,2,1,0:T(8,128)(2,1)S(1)}, f32[5,2,128,128]{3,2,1,0:T(8,128)S(1)}, f32[2,128,128]{2,1,0:T(8,128)S(1)}, f32[2,384,128]{2,1,0:T(8,1...) custom-call(s32[48]{0:T(128)S(1)} %copy-done.1, ...), custom_call_target="tpu_custom_call" | custom-call | tf_op jit(solution)/shard_map/local/pallas_call | solution.py:613
  13.5 0.0 copy-start.5
  13.5 0.0 copy-done.3
  13.5 0.0 copy-done.4
  13.5 0.7 copy-done.5
  14.2 63.6 %conditional.1 = ((bf16[2048,256]{1,0:T(8,128)(2,1)}, f32[3,2,128,128]{3,2,1,0:T(8,128)})) conditional(s32[]{:T(128)} %bitcast, (s32[5]{0:T(128)S(1)}, bf16[2048,256]{1,0:T(8,128)(2,1)}, bf16[2048,256]{1,0:T(8,128)(2,1)S(1)}, bf16[2048,256]{1,0:T(8,128)(2,1)S(1)}, bf16[8,2,128,256]{3,2,1,0:T(8,128)(2,1)S(1)}, ...), branch_computations={%region_0.0_spmd, %region_1.0_spmd, %region_2.0_spmd, %region_3.0_... | conditional | bytes 8 | solution.py:684
  14.2 62.0 %ring12.1 = (bf16[2048,256]{1,0:T(8,128)(2,1)S(1)}, f32[3,2,128,128]{3,2,1,0:T(8,128)S(1)}) custom-call(s32[5]{0:T(128)S(1)} %get-tuple-element.234.ends_s, bf16[2048,256]{1,0:T(8,128)(2,1)} %get-tuple-element.235.q_hbm, bf16[2048,256]{1,0:T(8,128)(2,1)S(1)} %get-tuple-element.236.k_hbm, bf16[2048,256]{1,0:T(8,128)(2,1)S(1)} %get-tuple-element.237.v_hbm, ...), custom_call_target="tpu_custom_call" | custom-call | tf_op jit(solution)/shard_map/cond/branch_3_fun/ring12/pallas_call | solution.py:682
  76.2 1.1 %store.11 = (bf16[2048,256]{1,0:T(8,128)(2,1)}, f32[3,2,128,128]{3,2,1,0:T(8,128)}) custom-call(bf16[2048,256]{1,0:T(8,128)(2,1)S(1)} %get-tuple-element.246.attended, f32[3,2,128,128]{3,2,1,0:T(8,128)S(1)} %get-tuple-element.247.final), custom_call_target="tpu_custom_call" | custom-call | tf_op jit(solution)/shard_map/cond/branch_3_fun/store/pallas_call | solution.py:682
Async XLA Ops:
  0.6 0.7 copy-start.2
  0.6 0.7 copy-start.1
  1.3 0.7 copy-start
  2.0 11.5 %copy-start.3 = (bf16[2048,256]{1,0:T(8,128)(2,1)S(1)}, bf16[2048,256]{1,0:T(8,128)(2,1)}, u32[]{:S(2)}) copy-start(bf16[2048,256]{1,0:T(8,128)(2,1)} %k_hbm.1) | copy-start | bytes 3145732
  2.0 11.5 %copy-start.4 = (bf16[2048,256]{1,0:T(8,128)(2,1)S(1)}, bf16[2048,256]{1,0:T(8,128)(2,1)}, u32[]{:S(2)}) copy-start(bf16[2048,256]{1,0:T(8,128)(2,1)} %v_hbm.1) | copy-start | bytes 3145732
  13.5 0.7 copy-start.5
where the time goes:
time: 79.3 us; the launch traced here: 78.1 us
  Pallas kernels  73.9 us (93%)
  local copies, waits for them, and re-layouts  2.03 us (3%)
  between operations  1.55 us (2%)
    pallas_call x2, Pallas kernels, exchange(): return lambda *operands: store_call(*ring_call(*operands))  63.1 us
    pallas_call x1, Pallas kernels, shards(): pl.pallas_call(functools.partial(local_kernel, ring), out_shape=(shape((c...  10.8 us
    unnamed x12, local copies, waits for them, and re-layouts  2.03 us

commit v1 on v0

--- a/solution.py
+++ b/solution.py
@@ -15,7 +15,7 @@
 LANES = 128
 LONGEST = 32
 LENGTHS = (9, 10, 11, 12, 13, 14, 16, LONGEST)
-PIECES = 4
+PIECES = 2
 FAR = 1 << 20
 NEG = -1e30
 EPSILON = 1e-06
@@ -36,10 +36,9 @@
     return jnp.concatenate([upper, lower], axis=axis)
 
 
-def outer_sum(scaled_keys, values):
-    both = lax.dot_general(
-        halves(scaled_keys, 1), values, (((0,), (0,)), ((), ())), preferred_element_type=F32
-    )
+def outer_sum(turned_keys, weight_row, values):
+    scaled = halves(turned_keys.astype(F32) * weight_row, 0)
+    both = jnp.dot(scaled, values, preferred_element_type=F32)
     return both[:DK] + both[DK:]
 
 
@@ -73,11 +72,11 @@
         owner, row = (item - 1) >> 2, (item - 1) & 3
         right = (owner - dev) & (ring - 1)
         left = (ring - right) & (ring - 1)
-        mixed_bits = ((item * 37 + candidate * 1013 + 7) * 40503) >> 9
-        draw = (mixed_bits ^ (mixed_bits >> 5)) & 7
-        free = draw < jnp.where(right == half - 1, 6, jnp.where(right == half, 4, 2))
+        mixed_bits = item * (2 * candidate + 1) * 40503 + candidate * 7919
+        draw = ((mixed_bits >> 11) ^ (mixed_bits >> 6)) & 31
+        free = draw < 16 + (half - right) * 5
         fixed = (right < half) | ((right == half) & ((item & 1) == 0))
-        near = (right >= half - 1) & (right <= half + 1) & (candidate > 0)
+        near = (right >= half - 3) & (right <= half + 3) & (candidate > 0)
         go_right = (near & free) | (jnp.logical_not(near) & fixed)
         turned = (go_right & jnp.logical_not(leftward)) | (jnp.logical_not(go_right) & leftward)
         chosen = (item > 0) & (right > 0) & turned
@@ -145,16 +144,14 @@
     return index
 
 
-def decay_parts(run_row, run_col, c, h, heads):
+def decay_row(run_row, c, h, heads):
     per = CHUNK // LANES
-    base = pl.multiple_of(c * CHUNK, CHUNK)
-    col = run_col[pl.ds(base, CHUNK), h : h + 1]
     row = jnp.concatenate(
         [run_row[pl.ds((per * c + i) * heads + h, 1), :] for i in range(per)], axis=1
     )
     prior = run_row[pl.ds(jnp.maximum(per * c - 1, 0) * heads + h, 1), :]
     at_entry = jnp.where(c > 0, prior[:, LANES - 1 :], 0.0)
-    return col, row, at_entry
+    return row, at_entry
 
 
 def local_kernel(
@@ -170,7 +167,6 @@
     table_ref,
     first_ref,
     run_row,
-    run_col,
     ends_out,
     branch_ref,
     len_ref,
@@ -179,6 +175,7 @@
     k_ref,
     v_ref,
     state,
+    keys_t,
     plan,
     finish_s,
     sems,
@@ -224,12 +221,6 @@
         earlier.astype(F32), totals, precision=PRECISE, preferred_element_type=F32
     )
     run_row[...] = running
-    turned = running.T
-    for c in range(tiles):
-        shift = (LANES - heads * c) % LANES
-        run_col[c * LANES : (c + 1) * LANES, :] = (
-            pltpu.roll(turned, shift, 1) if shift else turned
-        )
 
     total = jnp.int32(0)
     before = jnp.int32(0)
@@ -272,24 +263,26 @@
     def chunk(c, held):
         base = pl.multiple_of(c * CHUNK, CHUNK)
         span = pl.ds(base, CHUNK)
-        index_col = index_of(base + iota((CHUNK, 1), 0), ends)
+        index_row = index_of(base + iota((1, CHUNK), 1), ends)
         entry = index_of(base - 1, ends)
         last = index_of(base + CHUNK - 1, ends)
         following = []
         for h in range(heads):
             cols = slice(h * DK, (h + 1) * DK)
-            col, row, at_entry = decay_parts(run_row, run_col, c, h, heads)
+            row, at_entry = decay_row(run_row, c, h, heads)
             at_last = row[:, CHUNK - 1 :]
             state[c, h] = held[h]
             held_ref[c, h] = halves(held[h], 1)
-            weight = jnp.exp(jnp.where(index_col == last, at_last - col, NEG))
+            turned_keys = k_ref[span, cols].T
+            keys_t[c, h] = turned_keys
+            weight = jnp.exp(jnp.where(index_row == last, at_last - row, NEG))
             keep = jnp.exp(jnp.where(entry == last, at_last - at_entry, NEG))
-            fresh = outer_sum(k_ref[span, cols].astype(F32) * weight, v_ref[span, cols])
+            fresh = outer_sum(turned_keys, weight, v_ref[span, cols])
             following.append(keep * held[h] + fresh)
         return tuple(following)
 
     empty = tuple(jnp.zeros((DK, DV), F32) for _ in range(heads))
-    held = lax.fori_loop(0, tok // CHUNK, chunk, empty)
+    held = lax.fori_loop(0, tok // CHUNK, chunk, empty, unroll=2)
     open_end = index_of(jnp.int32(tok - 1), ends) == ended
     for h in range(heads):
         tail_ref[h] = jnp.where(open_end, held[h], 0.0)
@@ -299,16 +292,16 @@
         c = place // CHUNK
         base = pl.multiple_of(c * CHUNK, CHUNK)
         span = pl.ds(base, CHUNK)
-        index_col = index_of(base + iota((CHUNK, 1), 0), ends)
+        positions = base + iota((1, CHUNK), 1)
+        index_row = index_of(positions, ends)
         entry = index_of(base - 1, ends)
-        here = base + iota((1, CHUNK), 1) == place
         for h in range(heads):
             cols = slice(h * DK, (h + 1) * DK)
-            col, row, at_entry = decay_parts(run_row, run_col, c, h, heads)
-            at_end = jnp.sum(jnp.where(here, row, 0.0), axis=1, keepdims=True)
-            weight = jnp.exp(jnp.where(index_col == k, at_end - col, NEG))
+            row, at_entry = decay_row(run_row, c, h, heads)
+            at_end = jnp.sum(jnp.where(positions == place, row, 0.0), axis=1, keepdims=True)
+            weight = jnp.exp(jnp.where(index_row == k, at_end - row, NEG))
             keep = jnp.exp(jnp.where(entry == k, at_end - at_entry, NEG))
-            fresh = outer_sum(k_ref[span, cols].astype(F32) * weight, v_ref[span, cols])
+            fresh = outer_sum(keys_t[c, h], weight, v_ref[span, cols])
             ends_ref[k, h] = keep * state[c, h] + fresh
         return carry
 
@@ -332,7 +325,6 @@
     table_ref,
     first_ref,
     run_row,
-    run_col,
     gain_ref,
     attended_ref,
     final_ref,
@@ -340,6 +332,7 @@
     k_ref,
     v_ref,
     ends_ref,
+    run_col,
     mixed,
     sums,
     got,
@@ -438,6 +431,12 @@
         send_piece(1, 0, part, ends_in[0, part[0], part[2]], ends_in, 1)
     for k in range(1, ENDS):
         ends_ref[k] = ends_in[k]
+    turned = run_row[...].T
+    for c in range(tiles):
+        shift = (LANES - heads * c) % LANES
+        run_col[c * LANES : (c + 1) * LANES, :] = (
+            pltpu.roll(turned, shift, 1) if shift else turned
+        )
     for load in loads:
         load.wait()
     for h, i, rows in parts:
@@ -463,7 +462,8 @@
         linked = (index_col == index_row) & (iota(block, 0) >= iota(block, 1))
         for h in range(heads):
             cols = slice(h * DK, (h + 1) * DK)
-            col, row, at_entry = decay_parts(run_row, run_col, c, h, heads)
+            row, at_entry = decay_row(run_row, c, h, heads)
+            col = run_col[span, h : h + 1]
             query = q_ref[span, cols]
             scores = lax.dot_general(
                 query, k_ref[span, cols], (((1,), (1,)), ((), ())), preferred_element_type=F32
@@ -619,12 +619,11 @@
                 shape((2, table_rows(), LANES), F32),
                 shape((8, LANES), F32),
                 shape((LANES, LANES), F32),
-                shape((tok, LANES), F32),
                 shape((ENDS,), jnp.int32),
                 shape((1,), jnp.int32),
             ),
             in_specs=hbm(5),
-            out_specs=tuple(vmem(7)) + (smem, smem),
+            out_specs=tuple(vmem(6)) + (smem, smem),
             scratch_shapes=[
                 pltpu.SMEM((prompts,), jnp.int32),
                 pltpu.SMEM((prompts,), jnp.int32),
@@ -632,6 +631,7 @@
                 pltpu.VMEM((tok, width), BF16),
                 pltpu.VMEM((tok, width), BF16),
                 pltpu.VMEM((chunks, heads, DK, DV), F32),
+                pltpu.VMEM((chunks, heads, DK, CHUNK), BF16),
                 pltpu.VMEM((LONGEST, 8, LANES), jnp.int32),
                 pltpu.SMEM((prompts,), jnp.int32),
                 pltpu.SemaphoreType.DMA((5,)),
@@ -647,13 +647,14 @@
             ring_call = pl.pallas_call(
                 functools.partial(ring_kernel, steps, (ring, head_size)),
                 out_shape=outs,
-                in_specs=[smem] + hbm(3) + vmem(8),
+                in_specs=[smem] + hbm(3) + vmem(7),
                 out_specs=tuple(vmem(2)),
                 scratch_shapes=[
                     pltpu.VMEM((tok, width), BF16),
                     pltpu.VMEM((tok, width), BF16),
                     pltpu.VMEM((tok, width), BF16),
                     pltpu.VMEM((ENDS, heads, DK, DV), F32),
+                    pltpu.VMEM((tok, LANES), F32),
                     pltpu.VMEM((tok, width), F32),
                     pltpu.VMEM((4, tiles, LANES), F32),
                     pltpu.VMEM((max(hops, 1), tiles, LANES), F32),

time: 79.3 us -> 68.6 us (0.87)
  the two profiles are of different devices: /device:TPU:8 before, /device:TPU:4 now
where the time goes in v1:
time: 68.6 us; the launch traced here: 68.1 us
  Pallas kernels  64.3 us (94%)
  local copies, waits for them, and re-layouts  2.03 us (3%)
  between operations  1.51 us (2%)
    pallas_call x2, Pallas kernels, exchange(): return lambda *operands: store_call(*ring_call(*operands))  56.5 us
    pallas_call x1, Pallas kernels, shards(): pl.pallas_call(functools.partial(local_kernel, ring), out_shape=(shape((c...  7.81 us
    unnamed x12, local copies, waits for them, and re-layouts  2.03 us

profile of v1, /device:TPU:4, one launch (start us, length us, event | category | flops | bytes accessed | tf_op | source)
XLA Modules:
  0.0 68.1 jit_solution(14183366925290863751)
XLA Ops:
  0.6 0.0 copy-start.2
  0.6 0.0 copy-start.1
  0.7 0.6 copy-done.2
  1.3 0.0 copy-done.1
  1.3 0.0 copy-start
  1.3 0.7 %copy-done = f32[2,2048]{1,0:T(2,128)S(1)} copy-done((f32[2,2048]{1,0:T(2,128)S(1)}, f32[2,2048]{1,0:T(2,128)}, u32[]{:S(2)}) %copy-start) | copy-done | bytes 16408
  2.0 0.0 copy-start.3
  2.0 0.0 copy-start.4
  2.0 7.8 %local.1 = (bf16[8,2,128,256]{3,2,1,0:T(8,128)(2,1)S(1)}, f32[5,2,128,128]{3,2,1,0:T(8,128)S(1)}, f32[2,128,128]{2,1,0:T(8,128)S(1)}, f32[2,384,128]{2,1,0:T(8,1...) custom-call(s32[48]{0:T(128)S(1)} %copy-done.1, s32[48]{0:T(128)S(1)} %copy-done.2, ...), custom_call_target="tpu_custom_call" | custom-call | tf_op jit(solution)/shard_map/local/pallas_call | solution.py:613
  10.5 0.0 copy-start.5
  10.5 0.0 copy-done.3
  10.5 0.0 copy-done.4
  10.5 0.7 copy-done.5
  11.2 56.7 %conditional.1 = ((bf16[2048,256]{1,0:T(8,128)(2,1)}, f32[3,2,128,128]{3,2,1,0:T(8,128)})) conditional(s32[]{:T(128)} %bitcast, (s32[5]{0:T(128)S(1)}, bf16[2048,256]{1,0:T(8,128)(2,1)}, bf16[2048,256]{1,0:T(8,128)(2,1)S(1)}, bf16[2048,256]{1,0:T(8,128)(2,1)S(1)}, bf16[8,2,128,256]{3,2,1,0:T(8,128)(2,1)S(1)}, ...), branch_computations={%region_0.0_spmd, %region_1.0_spmd, %region_2.0_spmd, %region_3.0_... | conditional | bytes 8 | solution.py:685
  11.2 55.4 %ring11.1 = (bf16[2048,256]{1,0:T(8,128)(2,1)S(1)}, f32[3,2,128,128]{3,2,1,0:T(8,128)S(1)}) custom-call(s32[5]{0:T(128)S(1)} %get-tuple-element.202.ends_s, bf16[2048,256]{1,0:T(8,128)(2,1)} %get-tuple-element.203.q_hbm, bf16[2048,256]{1,0:T(8,128)(2,1)S(1)} %get-tuple-element.204.k_hbm, bf16[2048,256]{1,0:T(8,128)(2,1)S(1)} %get-tuple-element.205.v_hbm, ...), custom_call_target="tpu_custom_call" | custom-call | tf_op jit(solution)/shard_map/cond/branch_2_fun/ring11/pallas_call | solution.py:683
  66.5 1.1 %store.10 = (bf16[2048,256]{1,0:T(8,128)(2,1)}, f32[3,2,128,128]{3,2,1,0:T(8,128)}) custom-call(bf16[2048,256]{1,0:T(8,128)(2,1)S(1)} %get-tuple-element.213.attended, f32[3,2,128,128]{3,2,1,0:T(8,128)S(1)} %get-tuple-element.214.final), custom_call_target="tpu_custom_call" | custom-call | tf_op jit(solution)/shard_map/cond/branch_2_fun/store/pallas_call | solution.py:683
Async XLA Ops:
  0.6 0.7 copy-start.2
  0.6 0.7 copy-start.1
  1.3 0.7 %copy-start = (f32[2,2048]{1,0:T(2,128)S(1)}, f32[2,2048]{1,0:T(2,128)}, u32[]{:S(2)}) copy-start(f32[2,2048]{1,0:T(2,128)} %decay_hbm.1) | copy-start | bytes 49156
  2.0 8.5 %copy-start.3 = (bf16[2048,256]{1,0:T(8,128)(2,1)S(1)}, bf16[2048,256]{1,0:T(8,128)(2,1)}, u32[]{:S(2)}) copy-start(bf16[2048,256]{1,0:T(8,128)(2,1)} %k_hbm.1) | copy-start | bytes 3145732
  2.0 8.5 %copy-start.4 = (bf16[2048,256]{1,0:T(8,128)(2,1)S(1)}, bf16[2048,256]{1,0:T(8,128)(2,1)}, u32[]{:S(2)}) copy-start(bf16[2048,256]{1,0:T(8,128)(2,1)} %v_hbm.1) | copy-start | bytes 3145732
  10.5 0.7 %copy-start.5 = (f32[256]{0:T(256)S(1)}, f32[256]{0:T(256)}, u32[]{:S(2)}) copy-start(f32[256]{0:T(256)} %param.19) | copy-start | bytes 3076
